TPU v7x, 32 devices: a whole 2x2x4 slice. The times are simulated.
32 devices in a mesh: group: 2 (over y), expert: 4 (over z), tensor: 4 (over x, core).
Axes of the slice: x: 2, y: 2, z: 4, core: 2. Of those that a mesh axis runs over, the one named last changes fastest.
Arguments:
- tokens: bfloat16 [512, 4096], P(('group', 'expert'), 'tensor'), parts along dimension 0, may hold values from -400 to 400
- norm_gain: float32 [4096], replicated, may hold values from 0.1 to 1.9
- expert_ids: int32 [512, 8], P(('group', 'expert')), parts along dimension 0, may hold values from 0 to 63, all different within a row; in each aligned block of 64 rows (0 to 63, 64 to 127, ...) at most 16 rows name the same one
- gate_weights: float32 [512, 8], P(('group', 'expert')), parts along dimension 0, may hold values from 0.1 to 1
- gate_proj: bfloat16 [64, 768, 4096], P('expert', 'tensor'), may hold values from -0.09375 to 0.09375
- up_proj: bfloat16 [64, 768, 4096], P('expert', 'tensor'), may hold values from -0.09375 to 0.09375
- down_proj: bfloat16 [64, 4096, 768], P('expert', 'tensor'), may hold values from -0.21875 to 0.21875
Outputs:
- moe_out: bfloat16 [512, 4096], P(('group', 'expert'), 'tensor'), parts along dimension 0
There are 2 independent parts, one for each index of `group`. A program takes and returns all parts, laid end to end along the dimension named above; an argument that names none is the same for every part. Nothing has to cross between parts.
Inputs may be any that keep to these rules, and one draw needn't show every extreme that they name: `expert_ids`: each row names 8 different experts. Within the rows of one device (aligned blocks of 64 rows) no expert is named by more than 16 rows, a bound that some block reaches.
All inputs are finite; a program needn't handle non-finite values.
Results may differ from a plain program's by a relative error of at most 0.008.
Values may be sent and summed in bfloat16 or wider, within the bound.
No kernel may reach another device: no remote copies, remote signals or barrier semaphores. Data moves between devices by JAX's collectives and lax.ppermute only.
A program may use at most 128 MiB of HBM per device.

v0:
```python
import jax
import jax.numpy as jnp
from jax import lax
from jax.sharding import PartitionSpec as P

D = 4096
EXPERTS = 64
TOP = 8
CAP = 16
epsilon = 1e-06


def slot_places(expert_ids):
    flat_ids = expert_ids.reshape(-1)
    onehot = (flat_ids[:, None] == jnp.arange(EXPERTS, dtype=jnp.int32)[None, :]).astype(jnp.int32)
    before = jnp.cumsum(onehot, axis=0) - onehot
    inside = jnp.sum(onehot * before, axis=1)
    return flat_ids * CAP + inside


def expert_block(slot_rows, gate_proj, up_proj, down_proj):
    sources = slot_rows.shape[0]
    local_experts = slot_rows.shape[1]
    item_count = slot_rows.shape[2]
    gate_act = jnp.einsum(
        "slcd,lfd->lfsc", slot_rows, gate_proj, preferred_element_type=jnp.float32
    )
    up_act = jnp.einsum("slcd,lfd->lfsc", slot_rows, up_proj, preferred_element_type=jnp.float32)
    hidden = (jax.nn.silu(gate_act) * up_act).astype(jnp.bfloat16)
    hidden = hidden.reshape(local_experts, hidden.shape[1], sources * item_count)
    hidden_all = lax.all_gather(hidden, "tensor", axis=1, tiled=True)
    hidden_all = hidden_all.reshape(local_experts, hidden_all.shape[1], sources, item_count)
    result = jnp.einsum(
        "lfsc,ldf->slcd", hidden_all, down_proj, preferred_element_type=jnp.float32
    ).astype(jnp.bfloat16)
    return lax.all_to_all(result, "expert", split_axis=0, concat_axis=0, tiled=True)


def body(tokens, norm_gain, expert_ids, gate_weights, gate_proj, up_proj, down_proj):
    local_experts = gate_proj.shape[0]
    groups = lax.axis_size("expert")
    tok_rows = tokens.shape[0]
    places = slot_places(expert_ids)
    owners = (
        jnp.full((EXPERTS * CAP,), tok_rows, jnp.int32)
        .at[places]
        .set(jnp.arange(places.shape[0], dtype=jnp.int32) // TOP)
    )
    values = tokens.astype(jnp.float32)
    squares = lax.psum(jnp.sum(values * values, axis=1), "tensor")
    inv_scale = lax.rsqrt(squares / D + epsilon)[:, None]
    quarter_width = tokens.shape[1]
    gain_part = lax.dynamic_slice_in_dim(
        norm_gain, lax.axis_index("tensor") * quarter_width, quarter_width
    )
    normed = (values * inv_scale * gain_part).astype(jnp.bfloat16)
    padded = jnp.concatenate([normed, jnp.zeros((1, quarter_width), jnp.bfloat16)], axis=0)
    dispatched = padded[owners].reshape(groups, local_experts, CAP, quarter_width)
    full_rows = lax.all_gather(
        lax.all_to_all(dispatched, "expert", split_axis=0, concat_axis=0, tiled=True),
        "tensor",
        axis=3,
        tiled=True,
    )
    returned = expert_block(full_rows, gate_proj, up_proj, down_proj)
    out_width = returned.shape[-1]
    flat_back = returned.reshape(EXPERTS * CAP, out_width)
    picked = flat_back[places].reshape(tok_rows, TOP, out_width).astype(jnp.float32)
    return jnp.einsum("tkd,tk->td", picked, gate_weights).astype(jnp.bfloat16)


def solution(mesh):
    return jax.shard_map(
        body,
        mesh=mesh,
        in_specs=(
            P(("group", "expert"), "tensor"),
            P(),
            P(("group", "expert"), None),
            P(("group", "expert"), None),
            P("expert", "tensor", None),
            P("expert", "tensor", None),
            P("expert", "tensor", None),
        ),
        out_specs=P(("group", "expert"), "tensor"),
        check_vma=False,
    )
```

profile of v0, /device:TPU:0, one launch (start us, length us, event | category | flops | bytes accessed | tf_op | source)
XLA Modules:
  0.0 281.1 jit_solution(12578102919068015323)
XLA Ops:
  6.5 0.0 all-gather.3.cloned.1.call-start
  6.5 0.8 copy.15
  7.3 0.1 eq.29
  7.4 0.1 eq.25
  7.5 0.7 broadcast_multiply_fusion
  8.2 1.2 reduce-window.6
  9.4 0.2 slice_reduce_fusion
  9.7 0.1 copy.14
  9.8 0.1 mul.56
  9.9 0.1 fusion.27
  10.0 2.4 scatter_custom_fusion
  12.5 1.0 fusion.22
  13.5 8.4 %psum.7 = f32[64]{0:T(128)S(1)} all-reduce(f32[64]{0:T(128)S(1)} %fusion.22), channel_id=1, replica_groups=mesh['group'=2,'expert'=4,'tensor'=4] {'tensor'}, use_global_device_ids=true, to_apply=%region_1.2 | all-reduce | flops 64 | bytes 512 | tf_op jit(solution)/shard_map/psum | solution.py:50
  21.9 0.7 dynamic_slice.3
  22.6 1.0 fusion.24
  23.6 4.1 %gather_fusion = bf16[1024,1024]{1,0:T(8,128)(2,1)S(1)} fusion(bf16[65,1024]{1,0:T(8,128)(2,1)S(1)} %concatenate.3, s32[1024]{0:T(1024)S(1)} %fusion.29), kind=kCustom, calls=%fused_computation | custom fusion | bytes 4198400 | tf_op jit(solution)/shard_map/gather | solution.py:58
  27.7 51.7 %all_to_all.10 = bf16[4,16,16,1024]{3,2,1,0:T(8,128)(2,1)S(1)} all-to-all(bf16[4,16,16,1024]{3,2,1,0:T(8,128)(2,1)S(1)} %bitcast.72), channel_id=1, replica_groups=mesh['group'=2,'expert'=4,'tensor'=4] {'expert'}, dimensions={0} | all-to-all | bytes 4194304 | tf_op jit(solution)/shard_map/all_to_all | solution.py:60
  79.3 1.6 copy.18
  80.9 0.0 all-gather.3.cloned.1.call-update
  80.9 0.2 all-gather.5.cloned.1.call-start
  81.2 57.3 %all-gather.3.cloned.1.call-done = bf16[4,16,16,4096]{3,2,0,1:T(8,128)(2,1)} async-done(((bf16[4,16,16,1024]{3,2,0,1:T(8,128)(2,1)}), bf16[4,16,16,4096]{3,2,0,1:T(8,128)(2,1)}) %all-gather.3.cloned.1.call-update) | async-done | bytes 8388624 | tf_op jit(solution)/shard_map/all_gather | solution.py:59
  138.5 14.8 %fusion.8 = f32[16,192,4,16]{1,3,2,0:T(8,128)S(1)} fusion(bf16[4,16,16,4096]{3,2,0,1:T(8,128)(2,1)} %all-gather.3.cloned.1.call-done, bf16[16,192,4096]{2,1,0:T(8,128)(2,1)} %param.11), kind=kOutput, calls=%fused_computation.10 | convolution fusion | flops 1610612736 | bytes 34340864 | tf_op jit(solution)/shard_map/slcd,lfd->lfsc/dot_general | solution.py:25
  153.3 15.0 %fusion.17 = bf16[16,192,4,16]{1,3,2,0:T(8,128)(2,1)S(1)} fusion(bf16[4,16,16,4096]{3,2,0,1:T(8,128)(2,1)} %all-gather.3.cloned.1.call-done, bf16[16,192,4096]{2,1,0:T(8,128)(2,1)} %param.12, f32[16,192,4,16]{1,3,2,0:T(8,128)S(1)} %fusion.8), kind=kOutput, calls=%fused_computation.13 | convolution fusion | flops 1611792384 | bytes 34734080 | tf_op jit(solution)/shard_map/slcd,lfd->lfsc/dot_general | solution.py:28
  168.3 1.5 copy.19
  169.8 0.0 all-gather.5.cloned.1.call-update
  169.8 28.7 %all-gather.5.cloned.1.call-done = bf16[16,768,64]{2,0,1:T(8,128)(2,1)} async-done(((bf16[16,192,64]{2,0,1:T(8,128)(2,1)}), bf16[16,768,64]{2,0,1:T(8,128)(2,1)}) %all-gather.5.cloned.1.call-update) | async-done | bytes 1572880 | tf_op jit(solution)/shard_map/all_gather | solution.py:31
  198.5 5.0 %copy.20 = bf16[16,768,64]{1,2,0:T(8,128)(2,1)} copy(bf16[16,768,64]{2,0,1:T(8,128)(2,1)} %all-gather.5.cloned.1.call-done) | data formatting | bytes 3145728 | tf_op jit(solution)/shard_map/all_gather | solution.py:31
  203.5 12.8 %convert_bitcast_fusion = bf16[4,16,16,1024]{3,2,0,1:T(8,128)(2,1)S(1)} fusion(bf16[16,768,4,16]{1,3,2,0:T(8,128)(2,1)} %bitcast.73, bf16[16,1024,768]{2,1,0:T(8,128)(2,1)} %param.13), kind=kOutput, calls=%fused_computation.9 | convolution fusion | flops 1611661312 | bytes 28835840 | tf_op jit(solution)/shard_map/lfsc,ldf->slcd/dot_general | solution.py:33
  216.3 0.0 copy-start
  216.3 1.5 copy.21
  217.9 4.6 %all-to-all-start.1 = ((bf16[4,16,16,1024]{3,2,1,0:T(8,128)(2,1)}), bf16[4,16,16,1024]{3,2,1,0:T(8,128)(2,1)S(1)}, u32[]{:S(2)}, u32[]{:S(2)}) async-start(bf16[4,16,16,1024]{3,2,1,0:T(8,128)(2,1)} %copy.21), calls=%async_computation.1 | async-start | bytes 4194304 | tf_op jit(solution)/shard_map/all_to_all | solution.py:36
  222.5 0.0 copy-done
  222.5 0.1 copy.25
  222.6 48.5 %all-to-all-done.1 = bf16[4,16,16,1024]{3,2,1,0:T(8,128)(2,1)S(1)} async-done(((bf16[4,16,16,1024]{3,2,1,0:T(8,128)(2,1)}), bf16[4,16,16,1024]{3,2,1,0:T(8,128)(2,1)S(1)}, u32[]{:S(2)}, u32[]{:S(2)}) %all-to-all-start.1) | async-done | bytes 2097184 | tf_op jit(solution)/shard_map/all_to_all | solution.py:36
  271.1 2.0 gather_fusion.1
  273.1 0.4 fusion.20
  273.5 0.7 copy.30
  (9 shorter events, 0.1 us)
Async XLA Ops:
  6.5 132.0 %all-gather.3.cloned.1.call-start = ((), (), s32[]{:S(2)}) async-start(), calls=%async_computation.2 | async-start | bytes 10485760 | tf_op jit(solution)/shard_map/all_gather | solution.py:59
  80.9 117.5 %all-gather.5.cloned.1.call-start = ((), (), s32[]{:S(2)}) async-start(), calls=%async_computation.3 | async-start | bytes 3932160 | tf_op jit(solution)/shard_map/all_gather | solution.py:31
  216.3 6.2 %copy-start = (f32[64,8]{0,1:T(8,128)S(1)}, f32[64,8]{0,1:T(8,128)}, u32[]{:S(2)}) copy-start(f32[64,8]{0,1:T(8,128)} %param.10) | copy-start | bytes 6148
  217.9 53.2 %all-to-all-start.1 = ((bf16[4,16,16,1024]{3,2,1,0:T(8,128)(2,1)}), bf16[4,16,16,1024]{3,2,1,0:T(8,128)(2,1)S(1)}, u32[]{:S(2)}, u32[]{:S(2)}) async-start(bf16[4,16,16,1024]{3,2,1,0:T(8,128)(2,1)} %copy.21), calls=%async_computation.1 | async-start | bytes 4194304 | tf_op jit(solution)/shard_map/all_to_all | solution.py:36
Sparse Core Ops, SparseCore 0:
  81.1 57.3 all-gather.2
  169.9 28.4 all-gather.4
where the time goes:
time: 282 us; the launch traced here: 281 us
  waiting for transfers between devices  134 us (48%)
  blocking collectives  60 us (21%)
  matrix products  43.1 us (15%)
  local copies, waits for them, and re-layouts  21 us (7%)
  between operations  13.5 us (5%)
  starting transfers between devices  4.82 us (2%)
  other arithmetic  4.13 us (1%)
    all_gather x1, waiting for transfers between devices, body(): lax.all_gather(lax.all_to_all(dispatched, 'expert', split_axis=0, concat_...  57.3 us
    all_to_all x1, blocking collectives, body(): lax.all_to_all(dispatched, 'expert', split_axis=0, concat_axis=0, tiled=T...  51.7 us
    all_to_all x1, waiting for transfers between devices, expert_block(): lax.all_to_all(result, 'expert', split_axis=0, concat_axis=0, tiled=True)  48.5 us
    all_gather x1, waiting for transfers between devices, expert_block(): hidden_all = lax.all_gather(hidden, 'tensor', axis=1, tiled=True)  28.7 us
    dot_general x1, matrix products, expert_block(): jnp.einsum('slcd,lfd->lfsc', slot_rows, up_proj, preferred_element_type=j...  15 us
    dot_general x1, matrix products, expert_block(): jnp.einsum('slcd,lfd->lfsc', slot_rows, gate_proj, preferred_element_type...  14.8 us
    dot_general x1, matrix products, expert_block(): jnp.einsum('lfsc,ldf->slcd', hidden_all, down_proj, preferred_element_typ...  12.8 us
    psum x1, blocking collectives, body(): squares = lax.psum(jnp.sum(values * values, axis=1), 'tensor')  8.37 us
  transfers between devices with their start and end apart: 3, of which 3 were waited for; matrix products, arithmetic and copies ran while one was open for 0% of the time, Pallas kernels for 0%

commit v1 on v0

--- a/solution.py
+++ b/solution.py
@@ -28,7 +28,7 @@
     up_act = jnp.einsum("slcd,lfd->lfsc", slot_rows, up_proj, preferred_element_type=jnp.float32)
     hidden = (jax.nn.silu(gate_act) * up_act).astype(jnp.bfloat16)
     hidden = hidden.reshape(local_experts, hidden.shape[1], sources * item_count)
-    hidden_all = lax.all_gather(hidden, "tensor", axis=1, tiled=True)
+    hidden_all = jnp.concatenate(lax.all_gather(hidden, "tensor"), axis=1)
     hidden_all = hidden_all.reshape(local_experts, hidden_all.shape[1], sources, item_count)
     result = jnp.einsum(
         "lfsc,ldf->slcd", hidden_all, down_proj, preferred_element_type=jnp.float32

time: 282 us -> 276 us (0.979)
  waiting for transfers between devices: 134 us -> 129 us
    all_gather x1, waiting for transfers between devices: 28.7 us -> 22.7 us  [expert_block(): hidden_all = jnp.concatenate(lax.all_gather(hidden, 'tensor'), axis=1)]
    all_gather x1 -> x0, local copies, waits for them, and re-layouts: 4.99 us -> none  [expert_block(): hidden_all = lax.all_gather(hidden, 'tensor', axis=1, tiled=True)]
    another operation x1 -> x2, local copies, waits for them, and re-layouts: 0.01 us -> 2.86 us  [the longest x1 2.86 us: expert_block(): hidden_all.reshape(local_experts, hidden_all.shape[1], sources, item_count)]
where the time goes in v1:
time: 276 us
  waiting for transfers between devices  129 us (47%)
  blocking collectives  60 us (22%)
  matrix products  43.9 us (16%)
  local copies, waits for them, and re-layouts  20.8 us (8%)
  between operations  13.5 us (5%)
  starting transfers between devices  4.82 us (2%)
  other arithmetic  4.13 us (1%)
    all_gather x1, waiting for transfers between devices, body(): lax.all_gather(lax.all_to_all(dispatched, 'expert', split_axis=0, concat_...  57.3 us
    all_to_all x1, blocking collectives, body(): lax.all_to_all(dispatched, 'expert', split_axis=0, concat_axis=0, tiled=T...  51.7 us
    all_to_all x1, waiting for transfers between devices, expert_block(): lax.all_to_all(result, 'expert', split_axis=0, concat_axis=0, tiled=True)  48.5 us
    all_gather x1, waiting for transfers between devices, expert_block(): hidden_all = jnp.concatenate(lax.all_gather(hidden, 'tensor'), axis=1)  22.7 us
    dot_general x1, matrix products, expert_block(): jnp.einsum('slcd,lfd->lfsc', slot_rows, up_proj, preferred_element_type=j...  15.9 us
    dot_general x1, matrix products, expert_block(): jnp.einsum('slcd,lfd->lfsc', slot_rows, gate_proj, preferred_element_type...  14.8 us
    dot_general x1, matrix products, expert_block(): jnp.einsum('lfsc,ldf->slcd', hidden_all, down_proj, preferred_element_typ...  12.8 us
    psum x1, blocking collectives, body(): squares = lax.psum(jnp.sum(values * values, axis=1), 'tensor')  8.37 us
  transfers between devices with their start and end apart: 3, of which 3 were waited for; matrix products, arithmetic and copies ran while one was open for 0% of the time, Pallas kernels for 0%

profile of v1, /device:TPU:0, one launch (start us, length us, event | category | flops | bytes accessed | tf_op | source)
XLA Modules:
  0.0 275.7 jit_solution(10062662104745222131)
XLA Ops:
  6.5 0.0 all-gather.3.cloned.1.call-start
  6.5 0.8 copy.17
  7.3 0.1 eq.29
  7.4 0.1 eq.25
  7.5 0.7 broadcast_multiply_fusion
  8.2 1.2 reduce-window.6
  9.4 0.2 slice_reduce_fusion
  9.7 0.1 copy.16
  9.8 0.1 mul.56
  9.9 0.1 fusion.27
  10.0 2.4 scatter_custom_fusion
  12.5 1.0 fusion.22
  13.5 8.4 %psum.7 = f32[64]{0:T(128)S(1)} all-reduce(f32[64]{0:T(128)S(1)} %fusion.22), channel_id=1, replica_groups=mesh['group'=2,'expert'=4,'tensor'=4] {'tensor'}, use_global_device_ids=true, to_apply=%region_1.2 | all-reduce | flops 64 | bytes 512 | tf_op jit(solution)/shard_map/psum | solution.py:50
  21.9 0.7 dynamic_slice.3
  22.6 1.0 fusion.24
  23.6 4.1 %gather_fusion = bf16[1024,1024]{1,0:T(8,128)(2,1)S(1)} fusion(bf16[65,1024]{1,0:T(8,128)(2,1)S(1)} %concatenate.3, s32[1024]{0:T(1024)S(1)} %fusion.29), kind=kCustom, calls=%fused_computation | custom fusion | bytes 4198400 | tf_op jit(solution)/shard_map/gather | solution.py:58
  27.7 51.7 %all_to_all.10 = bf16[4,16,16,1024]{3,2,1,0:T(8,128)(2,1)S(1)} all-to-all(bf16[4,16,16,1024]{3,2,1,0:T(8,128)(2,1)S(1)} %bitcast.74), channel_id=1, replica_groups=mesh['group'=2,'expert'=4,'tensor'=4] {'expert'}, dimensions={0} | all-to-all | bytes 4194304 | tf_op jit(solution)/shard_map/all_to_all | solution.py:60
  79.3 1.6 copy.20
  80.9 0.0 all-gather.3.cloned.1.call-update
  80.9 0.2 all-gather.5.cloned.1.call-start
  81.2 57.3 %all-gather.3.cloned.1.call-done = bf16[4,16,16,4096]{3,2,0,1:T(8,128)(2,1)} async-done(((bf16[4,16,16,1024]{3,2,0,1:T(8,128)(2,1)}), bf16[4,16,16,4096]{3,2,0,1:T(8,128)(2,1)}) %all-gather.3.cloned.1.call-update) | async-done | bytes 8388624 | tf_op jit(solution)/shard_map/all_gather | solution.py:59
  138.5 14.8 %fusion.8 = f32[16,192,4,16]{1,3,2,0:T(8,128)S(1)} fusion(bf16[4,16,16,4096]{3,2,0,1:T(8,128)(2,1)} %all-gather.3.cloned.1.call-done, bf16[16,192,4096]{2,1,0:T(8,128)(2,1)} %param.11), kind=kOutput, calls=%fused_computation.10 | convolution fusion | flops 1610612736 | bytes 34340864 | tf_op jit(solution)/shard_map/slcd,lfd->lfsc/dot_general | solution.py:25
  153.3 15.9 %fusion.17 = bf16[16,192,4,16]{1,3,2,0:T(8,128)(2,1)} fusion(bf16[4,16,16,4096]{3,2,0,1:T(8,128)(2,1)} %all-gather.3.cloned.1.call-done, bf16[16,192,4096]{2,1,0:T(8,128)(2,1)} %param.12, f32[16,192,4,16]{1,3,2,0:T(8,128)S(1)} %fusion.8), kind=kOutput, calls=%fused_computation.13 | convolution fusion | flops 1611792384 | bytes 34734080 | tf_op jit(solution)/shard_map/slcd,lfd->lfsc/dot_general | solution.py:28
  169.1 0.0 all-gather.5.cloned.1.call-update
  169.2 22.7 %all-gather.5.cloned.1.call-done = bf16[4,16,192,64]{2,3,1,0:T(8,128)(2,1)} async-done(((bf16[1,16,192,64]{2,3,1,0:T(8,128)(2,1)}), bf16[4,16,192,64]{2,3,1,0:T(8,128)(2,1)}) %all-gather.5.cloned.1.call-update) | async-done | bytes 1572880 | tf_op jit(solution)/shard_map/all_gather | solution.py:31
  191.9 3.4 %copy.21 = bf16[16,4,192,64]{2,1,3,0:T(4,128)(2,1)S(1)} copy(bf16[16,4,192,64]{2,3,0,1:T(8,128)(2,1)} %bitcast.76) | data formatting | bytes 3145728 | tf_op jit(solution)/shard_map/reshape | solution.py:31
  195.2 2.9 %reshape_reshape.3 = bf16[16,768,4,16]{1,3,2,0:T(8,128)(2,1)} reshape(bf16[16,4,192,64]{2,1,3,0:T(4,128)(2,1)S(1)} %copy.21) | data formatting | bytes 3145728 | tf_op jit(solution)/shard_map/reshape;reshape | solution.py:32
  198.1 12.8 %convert_bitcast_fusion = bf16[4,16,16,1024]{3,2,0,1:T(8,128)(2,1)S(1)} fusion(bf16[16,768,4,16]{1,3,2,0:T(8,128)(2,1)} %reshape_reshape.3, bf16[16,1024,768]{2,1,0:T(8,128)(2,1)} %param.13), kind=kOutput, calls=%fused_computation.9 | convolution fusion | flops 1611661312 | bytes 28835840 | tf_op jit(solution)/shard_map/lfsc,ldf->slcd/dot_general | solution.py:33
  210.9 0.0 copy-start
  211.0 1.5 copy.22
  212.5 4.6 %all-to-all-start.1 = ((bf16[4,16,16,1024]{3,2,1,0:T(8,128)(2,1)}), bf16[4,16,16,1024]{3,2,1,0:T(8,128)(2,1)S(1)}, u32[]{:S(2)}, u32[]{:S(2)}) async-start(bf16[4,16,16,1024]{3,2,1,0:T(8,128)(2,1)} %copy.22), calls=%async_computation.1 | async-start | bytes 4194304 | tf_op jit(solution)/shard_map/all_to_all | solution.py:36
  217.1 0.0 copy-done
  217.1 0.1 copy.26
  217.2 48.5 %all-to-all-done.1 = bf16[4,16,16,1024]{3,2,1,0:T(8,128)(2,1)S(1)} async-done(((bf16[4,16,16,1024]{3,2,1,0:T(8,128)(2,1)}), bf16[4,16,16,1024]{3,2,1,0:T(8,128)(2,1)S(1)}, u32[]{:S(2)}, u32[]{:S(2)}) %all-to-all-start.1) | async-done | bytes 2097184 | tf_op jit(solution)/shard_map/all_to_all | solution.py:36
  265.7 2.0 gather_fusion.1
  267.7 0.4 fusion.20
  268.2 0.7 copy.31
  (9 shorter events, 0.1 us)
Async XLA Ops:
  6.5 132.0 %all-gather.3.cloned.1.call-start = ((), (), s32[]{:S(2)}) async-start(), calls=%async_computation.2 | async-start | bytes 10485760 | tf_op jit(solution)/shard_map/all_gather | solution.py:59
  80.9 110.9 %all-gather.5.cloned.1.call-start = ((), (), s32[]{:S(2)}) async-start(), calls=%async_computation.3 | async-start | bytes 2621440 | tf_op jit(solution)/shard_map/all_gather | solution.py:31
  210.9 6.2 %copy-start = (f32[64,8]{0,1:T(8,128)S(1)}, f32[64,8]{0,1:T(8,128)}, u32[]{:S(2)}) copy-start(f32[64,8]{0,1:T(8,128)} %param.10) | copy-start | bytes 6148
  212.5 53.2 %all-to-all-start.1 = ((bf16[4,16,16,1024]{3,2,1,0:T(8,128)(2,1)}), bf16[4,16,16,1024]{3,2,1,0:T(8,128)(2,1)S(1)}, u32[]{:S(2)}, u32[]{:S(2)}) async-start(bf16[4,16,16,1024]{3,2,1,0:T(8,128)(2,1)} %copy.22), calls=%async_computation.1 | async-start | bytes 4194304 | tf_op jit(solution)/shard_map/all_to_all | solution.py:36
Sparse Core Ops, SparseCore 0:
  81.1 57.3 all-gather.2
  169.3 22.5 all-gather.4
